TPU v7x, 256 devices: a whole 4x4x8 slice. The times are simulated.
256 devices in a mesh: grp: 16 (over y_hi, x, core), pose: 16 (over y_lo, z).
Axes of the slice: x: 4, y: 4 (y_hi: 2, y_lo: 2; y = y_hi * 2 + y_lo), z: 8, core: 2. Of those that a mesh axis runs over, the one named last changes fastest.
Arguments:
- particles: bfloat16 [81920, 16384], P(('grp', 'pose')), may hold values from -64 to 64
- projections: bfloat16 [128, 16384], P('pose'), may hold values from -1.5 to 1.5
- ctf_table: bfloat16 [32, 16384], replicated, may hold values from 0.099609375 to 1
- group_ids: int32 [81920], P(('grp', 'pose')), may hold values from 0 to 31
Outputs:
- gradient: float32 [128, 16384], P('pose', 'grp')
- log_norm: float32 [81920], P(('grp', 'pose'))
All inputs are finite; a program needn't handle non-finite values.
Results may differ from a plain program's by a relative error of at most 0.0065.
Values may be sent and summed in bfloat16 or wider, within the bound.
No kernel may reach another device: no remote copies, remote signals or barrier semaphores. Data moves between devices by JAX's collectives and lax.ppermute only.
A program may use at most 128 MiB of HBM per device.

v0:
```python
import math
import jax
import jax.numpy as jnp
from jax import lax
from jax.sharding import PartitionSpec as P


def shards(particles, projections, ctf_table, group_ids):
    high = lax.Precision.HIGHEST
    part_count = particles.shape[0]
    feature_count = particles.shape[1]
    group_count = ctf_table.shape[0]
    pose_local = projections.shape[0]
    pose_total = pose_local * lax.axis_size("pose")
    particle_total = part_count * lax.axis_size("grp") * lax.axis_size("pose")
    inverse = 4.0 / math.sqrt(feature_count)
    factor = pose_total / particle_total
    one_hot = (group_ids[:, None] == jnp.arange(group_count, dtype=jnp.int32)[None, :]).astype(
        jnp.bfloat16
    )
    one_hot_f32 = one_hot.astype(jnp.float32)
    ctf_rows = jnp.dot(one_hot, ctf_table, preferred_element_type=jnp.bfloat16)
    weighted = ctf_rows * particles
    ctf_square = jnp.square(ctf_table.astype(jnp.float32))
    gathered = lax.all_gather(projections, "pose", axis=0, tiled=True)
    raw_dots = lax.dot_general(
        weighted, gathered, (((1,), (1,)), ((), ())), preferred_element_type=jnp.float32
    )
    model_f32 = gathered.astype(jnp.float32)
    norms = lax.dot_general(
        ctf_square,
        model_f32 * model_f32,
        (((1,), (1,)), ((), ())),
        precision=high,
        preferred_element_type=jnp.float32,
    )
    picked = jnp.dot(one_hot_f32, norms, precision=high)
    scores = inverse * (raw_dots - 0.5 * picked)
    row_peak = jnp.max(scores, axis=1, keepdims=True)
    log_norm = row_peak[:, 0] + jnp.log(jnp.sum(jnp.exp(scores - row_peak), axis=1))
    weights = jnp.exp(scores - log_norm[:, None]).astype(jnp.bfloat16)
    pose_mass = lax.dot_general(
        weights, one_hot, (((0,), (0,)), ((), ())), preferred_element_type=jnp.float32
    )
    numerator = lax.dot_general(
        weights, weighted, (((0,), (0,)), ((), ())), preferred_element_type=jnp.float32
    )
    model_rows = gathered.astype(jnp.float32)
    numerator = numerator - model_rows * jnp.dot(pose_mass, ctf_square, precision=high)
    pose_share = lax.psum_scatter(factor * numerator, "pose", scatter_dimension=0, tiled=True)
    out_block = lax.psum_scatter(pose_share, "grp", scatter_dimension=1, tiled=True)
    return (out_block, log_norm)


def solution(mesh):
    return jax.shard_map(
        shards,
        mesh=mesh,
        in_specs=(P(("grp", "pose"), None), P("pose", None), P(), P(("grp", "pose"))),
        out_specs=(P("pose", "grp"), P(("grp", "pose"))),
        check_vma=False,
    )
```

profile of v0, /device:TPU:2, one launch (start us, length us, event | category | flops | bytes accessed | tf_op | source)
XLA Modules:
  0.0 300.7 jit_solution(8398676469700784404)
XLA Ops:
  7.2 0.0 all-gather.2.cloned.1.call-start
  7.2 0.7 all-gather.2.cloned.1.call-update
  7.9 0.0 copy-start.1
  7.9 0.0 reduce-scatter.3.cloned.1.call-start
  8.0 9.7 %convolution_multiply_fusion.1 = bf16[320,16384]{1,0:T(8,128)(2,1)} fusion(bf16[320,16384]{1,0:T(8,128)(2,1)} %param.4, bf16[32,16384]{1,0:T(8,128)(2,1)} %param.6, s32[320]{0:T(512)} %param.7), kind=kOutput, calls=%fused_computation.3 | convolution fusion | flops 340797440 | bytes 22021376 | tf_op jit(solution)/shard_map/dot_general | solution.py:22
  17.7 72.0 %all-gather.2.cloned.1.call-done = bf16[128,16384]{1,0:T(8,128)(2,1)} async-done(((bf16[8,16384]{1,0:T(8,128)(2,1)}), bf16[128,16384]{1,0:T(8,128)(2,1)}) %all-gather.2.cloned.1.call-update) | async-done | bytes 4194320 | tf_op jit(solution)/shard_map/all_gather | solution.py:25
  89.6 0.0 copy-done.1
  89.6 0.0 slice-start
  89.6 10.0 %fusion.2 = f32[32,128]{1,0:T(8,128)S(1)} fusion(bf16[128,16384]{1,0:T(8,128)(2,1)} %all-gather.2.cloned.1.call-done, bf16[32,16384]{1,0:T(8,128)(2,1)S(1)} %copy-done.1), kind=kOutput, calls=%fused_computation.5 | convolution fusion | flops 810549248 | bytes 5259264 | tf_op jit(solution)/shard_map/dot_general | solution.py:30
  99.6 0.0 copy-start.2
  99.6 0.0 slice-start.1
  99.6 0.0 slice-start.2
  99.7 7.0 %fusion.11 = f32[320,128]{1,0:T(8,128)S(1)} fusion(bf16[320,16384]{1,0:T(8,128)(2,1)} %convolution_multiply_fusion.1, bf16[128,16384]{1,0:T(8,128)(2,1)} %all-gather.2.cloned.1.call-done), kind=kOutput, calls=%fused_computation.20 | convolution fusion | flops 1342177280 | bytes 14843904 | tf_op jit(solution)/shard_map/dot_general | solution.py:26
  106.6 0.0 copy-done.2
  106.6 0.4 fusion.10
  107.0 0.2 exponential_reduce_fusion
  107.3 0.0 slice-done
  107.3 0.0 slice-done.1
  107.3 0.0 slice-done.2
  107.3 0.0 copy-start.3
  107.3 0.0 copy-start
  107.3 2.5 fusion.9
  109.8 0.0 copy-done.3
  109.8 0.3 fusion.5
  110.1 0.0 copy-done
  110.1 10.2 %fusion.1 = f32[128,16384]{1,0:T(8,128)} fusion(f32[128,16384]{1,0:T(8,128)S(1)} %fusion.9, f32[128,32]{1,0:T(8,128)S(1)} %fusion.5, bf16[128,16384]{1,0:T(8,128)(2,1)S(1)} %copy-done, bf16[32,16384]{1,0:T(8,128)(2,1)S(1)} %copy-done.1), kind=kOutput, calls=%fused_computation.2 | convolution fusion | flops 814743552 | bytes 22036480 | tf_op jit(solution)/shard_map/dot_general | solution.py:49
  120.4 0.0 reduce-scatter.3.cloned.1.call-update
  120.4 0.0 reduce-scatter.5.cloned.1.call-start
  120.4 98.7 %reduce-scatter.3.cloned.1.call-done = f32[8,16384]{1,0:T(8,128)} async-done(((f32[128,16384]{1,0:T(8,128)}), f32[8,16384]{1,0:T(8,128)}) %reduce-scatter.3.cloned.1.call-update) | async-done | bytes 524304 | tf_op jit(solution)/shard_map/reduce_scatter | solution.py:50
  219.1 0.0 reduce-scatter.5.cloned.1.call-update
  219.1 75.0 %reduce-scatter.5.cloned.1.call-done = f32[8,1024]{1,0:T(8,128)} async-done(((f32[8,16384]{1,0:T(8,128)}), f32[8,1024]{1,0:T(8,128)}) %reduce-scatter.5.cloned.1.call-update) | async-done | bytes 32784 | tf_op jit(solution)/shard_map/reduce_scatter | solution.py:51
  (2 shorter events, 0.0 us)
Async XLA Ops:
  7.2 82.5 %all-gather.2.cloned.1.call-start = ((), (), s32[]{:S(2)}) async-start(), calls=%async_computation.2 | async-start | bytes 4456448 | tf_op jit(solution)/shard_map/all_gather | solution.py:25
  7.9 81.7 %copy-start.1 = (bf16[32,16384]{1,0:T(8,128)(2,1)S(1)}, bf16[32,16384]{1,0:T(8,128)(2,1)}, u32[]{:S(2)}) copy-start(bf16[32,16384]{1,0:T(8,128)(2,1)} %param.6) | copy-start | bytes 3145732
  7.9 211.2 %reduce-scatter.3.cloned.1.call-start = ((), (), s32[]{:S(2)}) async-start(), calls=%async_computation.3 | async-start | bytes 8912896 | tf_op jit(solution)/shard_map/reduce_scatter | solution.py:50
  89.6 17.6 %slice-start = ((s8[10485760]{0:T(1024)(128)(4,1)}), s8[4194304]{0:T(1024)(128)(4,1)S(1)}, s32[]{:S(2)}) async-start(s8[10485760]{0:T(1024)(128)(4,1)} %bitcast.6), calls=%async_computation.5 | async-start | bytes 8388608
  99.6 7.0 %copy-start.2 = (s32[320]{0:T(512)S(1)}, s32[320]{0:T(512)}, u32[]{:S(2)}) copy-start(s32[320]{0:T(512)} %param.7) | copy-start | bytes 3844
  99.6 7.6 %slice-start.1 = ((s8[10485760]{0:T(1024)(128)(4,1)}), s8[4194304]{0:T(1024)(128)(4,1)S(1)}, s32[]{:S(2)}) async-start(s8[10485760]{0:T(1024)(128)(4,1)} %bitcast.6), calls=%async_computation.6 | async-start | bytes 8388608
  99.6 7.6 %slice-start.2 = ((s8[10485760]{0:T(1024)(128)(4,1)}), s8[2097152]{0:T(1024)(128)(4,1)S(1)}, s32[]{:S(2)}) async-start(s8[10485760]{0:T(1024)(128)(4,1)} %bitcast.6), calls=%async_computation.7 | async-start | bytes 4194304
  107.3 2.5 copy-start.3
  107.3 2.8 copy-start
  120.4 173.8 %reduce-scatter.5.cloned.1.call-start = ((), (), s32[]{:S(2)}) async-start(), calls=%async_computation.4 | async-start | bytes 557056 | tf_op jit(solution)/shard_map/reduce_scatter | solution.py:51
Sparse Core Ops, SparseCore 0:
  9.8 79.7 all-gather.1
  120.5 98.5 reduce-scatter.2
  223.8 70.3 reduce-scatter.4
where the time goes:
time: 301 us
  waiting for transfers between devices  246 us (82%)
  matrix products  40 us (13%)
  between operations  13.9 us (5%)
    reduce_scatter x1, waiting for transfers between devices, shards(): lax.psum_scatter(factor * numerator, 'pose', scatter_dimension=0, tiled=T...  98.7 us
    reduce_scatter x1, waiting for transfers between devices, shards(): lax.psum_scatter(pose_share, 'grp', scatter_dimension=1, tiled=True)  75 us
    all_gather x1, waiting for transfers between devices, shards(): gathered = lax.all_gather(projections, 'pose', axis=0, tiled=True)  72 us
    dot_general x1, matrix products, shards(): jnp.dot(pose_mass, ctf_square, precision=high)  10.2 us
    dot_general x1, matrix products, shards(): lax.dot_general(ctf_square, model_f32 * model_f32, (((1,), (1,)), ((), ()...  9.99 us
    dot_general x1, matrix products, shards(): ctf_rows = jnp.dot(one_hot, ctf_table, preferred_element_type=jnp.bfloat16)  9.71 us
    dot_general x1, matrix products, shards(): lax.dot_general(weighted, gathered, (((1,), (1,)), ((), ())), preferred_e...  6.95 us
  transfers between devices with their start and end apart: 3, of which 3 were waited for; matrix products, arithmetic and copies ran while one was open for 3% of the time, Pallas kernels for 0%

commit v1 on v0

--- a/solution.py
+++ b/solution.py
@@ -22,7 +22,15 @@
     ctf_rows = jnp.dot(one_hot, ctf_table, preferred_element_type=jnp.bfloat16)
     weighted = ctf_rows * particles
     ctf_square = jnp.square(ctf_table.astype(jnp.float32))
-    gathered = lax.all_gather(projections, "pose", axis=0, tiled=True)
+    gathered = jnp.concatenate(
+        lax.all_to_all(
+            jnp.stack([projections for _ in range(lax.axis_size("pose"))], axis=0),
+            axis_name="pose",
+            split_axis=0,
+            concat_axis=0,
+        ),
+        0,
+    )
     raw_dots = lax.dot_general(
         weighted, gathered, (((1,), (1,)), ((), ())), preferred_element_type=jnp.float32
     )

time: 301 us -> 332 us (1.10)
  waiting for transfers between devices: 246 us -> 265 us
  starting transfers between devices: 0.12 us -> 9.72 us
  local copies, waits for them, and re-layouts: 0.03 us -> 3.45 us
    all_to_all x0 -> x1, waiting for transfers between devices: none -> 87.1 us  [shards(): lax.all_to_all(jnp.stack([projections for _ in range(lax.axis_size('pose'...]
    all_gather x1 -> x0, waiting for transfers between devices: 72 us -> none  [shards(): gathered = lax.all_gather(projections, 'pose', axis=0, tiled=True)]
    all_to_all x0 -> x1, starting transfers between devices: none -> 9.63 us  [shards(): lax.all_to_all(jnp.stack([projections for _ in range(lax.axis_size('pose'...]
    reduce_scatter x1, waiting for transfers between devices: 98.7 us -> 103 us  [shards(): lax.psum_scatter(factor * numerator, 'pose', scatter_dimension=0, tiled=T...]
    another operation x0 -> x1, local copies, waits for them, and re-layouts: none -> 3.42 us  [shards(): jnp.stack([projections for _ in range(lax.axis_size('pose'))], axis=0)]
  transfers between devices with their start and end apart: 3 -> 3, of which waited for: 3 -> 3; matrix products, arithmetic and copies ran while one was open for 3% -> 2% of each run, Pallas kernels for 0% -> 0%
where the time goes in v1:
time: 332 us
  waiting for transfers between devices  265 us (80%)
  matrix products  39.8 us (12%)
  between operations  14.2 us (4%)
  starting transfers between devices  9.72 us (3%)
  local copies, waits for them, and re-layouts  3.45 us (1%)
    reduce_scatter x1, waiting for transfers between devices, shards(): lax.psum_scatter(factor * numerator, 'pose', scatter_dimension=0, tiled=T...  103 us
    all_to_all x1, waiting for transfers between devices, shards(): lax.all_to_all(jnp.stack([projections for _ in range(lax.axis_size('pose'...  87.1 us
    reduce_scatter x1, waiting for transfers between devices, shards(): lax.psum_scatter(pose_share, 'grp', scatter_dimension=1, tiled=True)  75 us
    dot_general x1, matrix products, shards(): jnp.dot(pose_mass, ctf_square, precision=high)  11.7 us
    dot_general x1, matrix products, shards(): lax.dot_general(ctf_square, model_f32 * model_f32, (((1,), (1,)), ((), ()...  10 us
    all_to_all x1, starting transfers between devices, shards(): lax.all_to_all(jnp.stack([projections for _ in range(lax.axis_size('pose'...  9.63 us
    dot_general x1, matrix products, shards(): ctf_rows = jnp.dot(one_hot, ctf_table, preferred_element_type=jnp.bfloat16)  8.04 us
    dot_general x1, matrix products, shards(): lax.dot_general(weighted, gathered, (((1,), (1,)), ((), ())), preferred_e...  6.96 us
  transfers between devices with their start and end apart: 3, of which 3 were waited for; matrix products, arithmetic and copies ran while one was open for 2% of the time, Pallas kernels for 0%

profile of v1, /device:TPU:2, one launch (start us, length us, event | category | flops | bytes accessed | tf_op | source)
XLA Modules:
  0.0 332.2 jit_solution(8731149569727703902)
XLA Ops:
  7.2 0.0 copy-start.1
  7.2 0.0 copy-start
  7.2 3.4 %stack.2 = bf16[16,8,16384]{2,1,0:T(8,128)(2,1)} broadcast(bf16[8,16384]{1,0:T(8,128)(2,1)} %param.5), dimensions={1,2} | broadcast | bytes 4456448 | tf_op jit(solution)/shard_map/stack | solution.py:27
  10.6 9.6 %all-to-all-start = ((bf16[16,8,16384]{2,1,0:T(8,128)(2,1)}), bf16[16,8,16384]{2,1,0:T(8,128)(2,1)}, u32[]{:S(2)}, u32[]{:S(2)}) async-start(bf16[16,8,16384]{2,1,0:T(8,128)(2,1)} %stack.2), calls=%async_computation | async-start | bytes 8388608 | tf_op jit(solution)/shard_map/all_to_all | solution.py:26
  20.2 0.0 reduce-scatter.3.cloned.1.call-start
  20.3 0.0 copy-done.1
  20.3 0.0 copy-done
  20.3 8.0 %convolution_multiply_fusion.1 = bf16[320,16384]{1,0:T(8,128)(2,1)} fusion(bf16[320,16384]{1,0:T(8,128)(2,1)} %param.4, bf16[32,16384]{1,0:T(8,128)(2,1)S(1)} %copy-done, s32[320]{0:T(512)S(1)} %copy-done.1), kind=kOutput, calls=%fused_computation.3 | convolution fusion | flops 340797440 | bytes 22021376 | tf_op jit(solution)/shard_map/dot_general | solution.py:22
  28.4 87.1 %all-to-all-done = bf16[16,8,16384]{2,1,0:T(8,128)(2,1)} async-done(((bf16[16,8,16384]{2,1,0:T(8,128)(2,1)}), bf16[16,8,16384]{2,1,0:T(8,128)(2,1)}, u32[]{:S(2)}, u32[]{:S(2)}) %all-to-all-start) | async-done | bytes 4194336 | tf_op jit(solution)/shard_map/all_to_all | solution.py:26
  115.5 0.0 slice-start
  115.5 10.0 %fusion.2 = f32[32,128]{1,0:T(8,128)S(1)} fusion(bf16[16,8,16384]{2,1,0:T(8,128)(2,1)} %all-to-all-done, bf16[32,16384]{1,0:T(8,128)(2,1)S(1)} %copy-done), kind=kOutput, calls=%fused_computation.5 | convolution fusion | flops 810549248 | bytes 5259264 | tf_op jit(solution)/shard_map/dot_general | solution.py:38
  125.5 0.0 slice-start.1
  125.5 0.0 slice-start.2
  125.5 7.0 %fusion.4 = f32[320,128]{1,0:T(8,128)S(1)} fusion(bf16[320,16384]{1,0:T(8,128)(2,1)} %convolution_multiply_fusion.1, bf16[16,8,16384]{2,1,0:T(8,128)(2,1)} %all-to-all-done), kind=kOutput, calls=%fused_computation.7 | convolution fusion | flops 1342177280 | bytes 14843904 | tf_op jit(solution)/shard_map/dot_general | solution.py:34
  132.4 0.4 fusion.13
  132.8 0.2 exponential_reduce_fusion
  133.1 0.0 slice-done
  133.1 0.0 slice-done.1
  133.1 0.0 slice-done.2
  133.1 0.0 copy-start.2
  133.1 2.5 fusion.12
  135.6 0.0 copy-done.2
  135.6 0.3 fusion.8
  135.9 11.7 %fusion.1 = f32[128,16384]{1,0:T(8,128)} fusion(f32[128,16384]{1,0:T(8,128)S(1)} %fusion.12, f32[128,32]{1,0:T(8,128)S(1)} %fusion.8, bf16[16,8,16384]{2,1,0:T(8,128)(2,1)} %all-to-all-done, bf16[32,16384]{1,0:T(8,128)(2,1)S(1)} %copy-done), kind=kOutput, calls=%fused_computation.2 | convolution fusion | flops 814743552 | bytes 22036480 | tf_op jit(solution)/shard_map/dot_general | solution.py:57
  147.6 0.0 reduce-scatter.3.cloned.1.call-update
  147.6 0.0 reduce-scatter.5.cloned.1.call-start
  147.7 102.6 %reduce-scatter.3.cloned.1.call-done = f32[8,16384]{1,0:T(8,128)} async-done(((f32[128,16384]{1,0:T(8,128)}), f32[8,16384]{1,0:T(8,128)}) %reduce-scatter.3.cloned.1.call-update) | async-done | bytes 524304 | tf_op jit(solution)/shard_map/reduce_scatter | solution.py:58
  250.3 0.0 reduce-scatter.5.cloned.1.call-update
  250.3 75.0 %reduce-scatter.5.cloned.1.call-done = f32[8,1024]{1,0:T(8,128)} async-done(((f32[8,16384]{1,0:T(8,128)}), f32[8,1024]{1,0:T(8,128)}) %reduce-scatter.5.cloned.1.call-update) | async-done | bytes 32784 | tf_op jit(solution)/shard_map/reduce_scatter | solution.py:59
  (2 shorter events, 0.0 us)
Async XLA Ops:
  7.2 13.1 %copy-start.1 = (s32[320]{0:T(512)S(1)}, s32[320]{0:T(512)}, u32[]{:S(2)}) copy-start(s32[320]{0:T(512)} %param.7) | copy-start | bytes 3844
  7.2 13.1 %copy-start = (bf16[32,16384]{1,0:T(8,128)(2,1)S(1)}, bf16[32,16384]{1,0:T(8,128)(2,1)}, u32[]{:S(2)}) copy-start(bf16[32,16384]{1,0:T(8,128)(2,1)} %param.6) | copy-start | bytes 3145732
  10.6 104.8 %all-to-all-start = ((bf16[16,8,16384]{2,1,0:T(8,128)(2,1)}), bf16[16,8,16384]{2,1,0:T(8,128)(2,1)}, u32[]{:S(2)}, u32[]{:S(2)}) async-start(bf16[16,8,16384]{2,1,0:T(8,128)(2,1)} %stack.2), calls=%async_computation | async-start | bytes 8388608 | tf_op jit(solution)/shard_map/all_to_all | solution.py:26
  20.2 230.0 %reduce-scatter.3.cloned.1.call-start = ((), (), s32[]{:S(2)}) async-start(), calls=%async_computation.3 | async-start | bytes 8912896 | tf_op jit(solution)/shard_map/reduce_scatter | solution.py:58
  115.5 17.6 %slice-start = ((s8[10485760]{0:T(1024)(128)(4,1)}), s8[4194304]{0:T(1024)(128)(4,1)S(1)}, s32[]{:S(2)}) async-start(s8[10485760]{0:T(1024)(128)(4,1)} %bitcast.13), calls=%async_computation.5 | async-start | bytes 8388608
  125.5 7.6 %slice-start.1 = ((s8[10485760]{0:T(1024)(128)(4,1)}), s8[4194304]{0:T(1024)(128)(4,1)S(1)}, s32[]{:S(2)}) async-start(s8[10485760]{0:T(1024)(128)(4,1)} %bitcast.13), calls=%async_computation.6 | async-start | bytes 8388608
  125.5 7.6 %slice-start.2 = ((s8[10485760]{0:T(1024)(128)(4,1)}), s8[2097152]{0:T(1024)(128)(4,1)S(1)}, s32[]{:S(2)}) async-start(s8[10485760]{0:T(1024)(128)(4,1)} %bitcast.13), calls=%async_computation.7 | async-start | bytes 4194304
  133.1 2.5 copy-start.2
  147.6 177.7 %reduce-scatter.5.cloned.1.call-start = ((), (), s32[]{:S(2)}) async-start(), calls=%async_computation.4 | async-start | bytes 557056 | tf_op jit(solution)/shard_map/reduce_scatter | solution.py:59
Sparse Core Ops, SparseCore 0:
  147.8 102.4 reduce-scatter.2
  254.9 70.3 reduce-scatter.4
